TPU v7x, 128 devices: a whole 4x4x4 slice. The times are simulated.
128 devices in a mesh: role: 2 (over y_hi), dp: 4 (over y_lo, core), ctx: 16 (over x, z).
Axes of the slice: x: 4, y: 4 (y_hi: 2, y_lo: 2; y = y_hi * 2 + y_lo), z: 4, core: 2. Of those that a mesh axis runs over, the one named last changes fastest.
Arguments:
- teacher_states: bfloat16 [4, 2048, 5120], P('dp', 'ctx'), may hold values from -50 to 50
- student_states: bfloat16 [4, 2048, 3584], P('dp', 'ctx'), may hold values from -50 to 50
- teacher_gain: float32 [5120], replicated, may hold values from 0.25 to 1.75
- student_gain: float32 [3584], replicated, may hold values from 0.25 to 1.75
- mentor_output_weights: bfloat16 [4, 5120, 2048], P(None, None, 'ctx'), may hold values from -2 to 2
- student_heads: bfloat16 [4, 3584, 2048], P(None, None, 'ctx'), may hold values from -2 to 2
- segments: int32 [4, 2048], P('dp', 'ctx'), may hold values from 0 to 31, never falling along the last dimension, each value on 1 to 256 neighbouring positions
- targets: int32 [4, 2048, 4], P('dp', 'ctx'), may hold values from 0 to 2047
Outputs:
- grad_heads: float32 [4, 3584, 2048], P(None, ('role', 'dp'), 'ctx')
- frame_terms: float32 [2, 4, 2048, 4], P('role', 'dp', 'ctx')
All inputs are finite; a program needn't handle non-finite values.
Results may differ from a plain program's by a relative error of at most 0.0048.
Values may be sent and summed in bfloat16 or wider, within the bound.
No kernel may reach another device: no remote copies, remote signals or barrier semaphores. Data moves between devices by JAX's collectives and lax.ppermute only.
A program may use at most 192 MiB of HBM per device.

v0:
```python
import jax
import jax.numpy as jnp
from jax import lax
from jax.sharding import Mesh
from jax.sharding import PartitionSpec as P

QUANTIZER_TOTAL = 4
MBATCH = 4
CTX = ("ctx_0", "ctx_1")
epsilon = 1e-06
sharpness_divisor = 2.0
blend_ratio = 0.5


def sent_together(arrays, axis, dim, along):
    columns = [a.reshape(*a.shape[:along], -1) for a in arrays]
    both = jnp.concatenate(columns, axis=along)
    filled, at, done = (lax.all_gather(both, axis, axis=dim, tiled=True), 0, [])
    for a, column in zip(arrays, columns):
        share = filled[..., at : at + column.shape[along]]
        done.append(share.reshape(*share.shape[:along], *a.shape[along:]))
        at += column.shape[along]
    return tuple(done)


def copy_for_each(array, axis):
    copies = jnp.broadcast_to(array, (lax.axis_size(axis), *array.shape))
    return lax.all_to_all(copies, axis, split_axis=0, concat_axis=0, tiled=True)


def collected_together(array, axis):
    leaves = jax.tree.leaves(array)
    turns = sorted(range(len(leaves)), key=lambda k: -leaves[k].size)
    width = (1, *leaves[turns[0]].shape)[-1]
    lines = [
        jnp.pad(leaves[k].reshape(-1), (0, -leaves[k].size % width)).reshape(-1, width)
        for k in turns
    ]
    both, at, found = (copy_for_each(jnp.concatenate(lines), axis), 0, {})
    for k, line in zip(turns, lines):
        share = both[:, at : at + len(line)].reshape(len(both), -1)
        found[k] = share[:, : leaves[k].size].reshape(-1, *leaves[k].shape)
        at += len(line)
    numbers = iter(range(len(leaves)))
    return jax.tree.map(lambda _: found[next(numbers)], array)


def joined_by_halves(pieces, combine):
    while len(jax.tree.leaves(pieces)[0]) > 1:
        pieces = jax.vmap(combine)(
            *(jax.tree.map(lambda part: part[side::2], pieces) for side in (0, 1))
        )
    return jax.tree.map(lambda part: part[0], pieces)


def combined_all(array, axis, combine):
    pieces = collected_together(array, axis)
    return joined_by_halves(pieces, combine)


def cut_along(array, dim, length):
    lengths = array.shape
    pieces = array.reshape(*lengths[:dim], length, lengths[dim] // length, *lengths[dim + 1 :])
    return jnp.moveaxis(pieces, dim, 0)


def sum_at_owner(array, axis, dim):
    length = lax.axis_size(axis)
    pieces = lax.all_to_all(cut_along(array, dim, length), axis, 0, 0, tiled=True)
    return jnp.sum(pieces, axis=0)


def whole_of(array, axes, dim):
    filled = array
    for number in range(len(axes) - 1, -1, -1):
        filled = lax.all_gather(filled, axes[number], axis=dim, tiled=True)
    return filled


def shifted(value, axis, steps):
    count = lax.axis_size(axis)
    initial, last = (max(0, -steps), min(count, count - steps))
    return lax.ppermute(value, axis, [(source, source + steps) for source in range(initial, last)])


def normalize(states, gain):
    values = states.astype(jnp.float32)
    factor = lax.rsqrt(jnp.mean(values * values, axis=-1, keepdims=True) + epsilon)
    return (values * factor * gain).astype(jnp.bfloat16)


def merge_teacher(first, second):
    largest_activation = jnp.maximum(first[0], second[0])
    return (
        largest_activation,
        first[1] * jnp.exp(first[0] - largest_activation)
        + second[1] * jnp.exp(second[0] - largest_activation),
    )


def merge_student(first, second):
    largest_activation = jnp.maximum(first[0], second[0])
    return (
        largest_activation,
        first[1] * jnp.exp(first[0] - largest_activation)
        + second[1] * jnp.exp(second[0] - largest_activation),
        first[2] * jnp.exp((first[0] - largest_activation) / sharpness_divisor)
        + second[2] * jnp.exp((second[0] - largest_activation) / sharpness_divisor),
    )


def on_device(
    teacher_states,
    student_states,
    teacher_gain,
    student_gain,
    mentor_output_weights,
    student_heads,
    segments,
    targets,
):
    columns = mentor_output_weights.shape[2]
    ctx_count = lax.axis_size(CTX)
    ctx_rank = lax.axis_index(CTX)
    col_start = ctx_rank * columns
    rows_here = teacher_states.shape[1]
    batch_rows = rows_here // MBATCH
    group_rows = batch_rows * ctx_count
    all_segments, all_targets = sent_together((segments, targets), CTX, 1, 2)
    length = all_segments.shape[1]
    documents = 2 * ctx_count
    members = (all_segments[0][None, :] == jnp.arange(documents, dtype=jnp.int32)[:, None]).astype(
        jnp.float32
    )
    counts = jnp.sum(members, axis=1)
    row_sizes = jnp.dot(counts, members, precision=lax.Precision.HIGHEST)
    weights = length / (documents * row_sizes)
    own_targets = all_targets[0] - col_start
    is_teacher = lax.axis_index("role") == 0
    positions = jnp.arange(columns)

    def per_batch(values, batch_index):
        trailing = values.shape[1:]
        return values.reshape((ctx_count, MBATCH, batch_rows) + trailing)[:, batch_index].reshape(
            (group_rows,) + trailing
        )

    gradient = jnp.zeros((QUANTIZER_TOTAL, student_heads.shape[1], columns), jnp.float32)
    frame_parts = []
    blocks = []
    teacher_parts = []
    for batch_index in range(MBATCH):
        teacher_local_rows = normalize(
            teacher_states[0, batch_index * batch_rows : (batch_index + 1) * batch_rows],
            teacher_gain,
        )
        scaled = (
            lax.cond(
                is_teacher,
                lambda piece: jnp.einsum(
                    "rd,qdc->rqc", piece, mentor_output_weights, preferred_element_type=jnp.float32
                ),
                lambda piece: jnp.zeros((piece.shape[0], QUANTIZER_TOTAL, columns), jnp.float32),
                lax.all_gather(teacher_local_rows, CTX, axis=0, tiled=True),
            )
            / sharpness_divisor
        )
        teacher_local_peak = jnp.max(scaled, axis=2)
        teacher_largest_activation, totals = combined_all(
            (teacher_local_peak, jnp.sum(jnp.exp(scaled - teacher_local_peak[:, :, None]), axis=2)),
            CTX,
            merge_teacher,
        )
        log_probs = scaled - (teacher_largest_activation + jnp.log(totals))[:, :, None]
        teacher_hits = positions[None, None, :] == per_batch(own_targets, batch_index)[:, :, None]
        picked = -jnp.sum(jnp.where(teacher_hits, log_probs, 0.0), axis=2)
        teacher_terms = sum_at_owner(picked, CTX, 0)
        block = log_probs.astype(jnp.bfloat16)
        blocks.append(block)
        teacher_parts.append(teacher_terms)
    arrived = shifted(jnp.stack(blocks), "role", 1)
    for batch_index in range(MBATCH):
        received = arrived[batch_index]
        student_gradient = gradient
        local_rows = normalize(
            student_states[0, batch_index * batch_rows : (batch_index + 1) * batch_rows],
            student_gain,
        )
        gathered = whole_of(local_rows, CTX, 0)
        raw_activation_grid = lax.cond(
            is_teacher,
            lambda rows: jnp.zeros((rows.shape[0], QUANTIZER_TOTAL, columns), jnp.float32),
            lambda rows: jnp.einsum(
                "rd,qdc->rqc", rows, student_heads, preferred_element_type=jnp.float32
            ),
            gathered,
        )
        local_peak = jnp.max(raw_activation_grid, axis=2)
        centered_activations = raw_activation_grid - local_peak[:, :, None]
        largest_activation, plain, warmed_totals = combined_all(
            (
                local_peak,
                jnp.sum(jnp.exp(centered_activations), axis=2),
                jnp.sum(jnp.exp(centered_activations / sharpness_divisor), axis=2),
            ),
            CTX,
            merge_student,
        )
        untempered_logdensity = (
            raw_activation_grid - (largest_activation + jnp.log(plain))[:, :, None]
        )
        warmed_logdensity = (
            raw_activation_grid / sharpness_divisor
            - (largest_activation / sharpness_divisor + jnp.log(warmed_totals))[:, :, None]
        )
        teacher_logp = received.astype(jnp.float32)
        mentor_distribution = jnp.exp(teacher_logp)
        hits = (positions[None, None, :] == per_batch(own_targets, batch_index)[:, :, None]).astype(
            jnp.float32
        )
        kullback_gap = jnp.sum(mentor_distribution * (teacher_logp - warmed_logdensity), axis=2)
        mismatch_penalty = -jnp.sum(hits * untempered_logdensity, axis=2)
        loss_values = (
            blend_ratio * sharpness_divisor * sharpness_divisor * kullback_gap
            + (1.0 - blend_ratio) * mismatch_penalty
        )
        terms = sum_at_owner(loss_values, CTX, 0)
        gradient_scaling = per_batch(weights, batch_index)[:, None, None] * (
            blend_ratio * sharpness_divisor * (jnp.exp(warmed_logdensity) - mentor_distribution)
            + (1.0 - blend_ratio) * (jnp.exp(untempered_logdensity) - hits)
        )
        gradient_scaling = gradient_scaling.astype(jnp.bfloat16)
        student_gradient = lax.cond(
            is_teacher,
            lambda total: total,
            lambda total: total
            + jnp.einsum(
                "rd,rqc->qdc", gathered, gradient_scaling, preferred_element_type=jnp.float32
            ),
            student_gradient,
        )
        gradient = student_gradient
        frame_parts.append(jnp.where(is_teacher, teacher_parts[batch_index], terms))
    shares = lax.psum_scatter(gradient, ("role", "dp"), scatter_dimension=1, tiled=True)
    frame_terms = jnp.concatenate(frame_parts, axis=0).reshape(1, 1, rows_here, QUANTIZER_TOTAL)
    return (shares, frame_terms)


def solution(mesh):
    finer = Mesh(
        mesh.devices.reshape(mesh.shape["role"], mesh.shape["dp"], 4, 4),
        ("role", "dp", "ctx_0", "ctx_1"),
    )
    placed = (
        P("dp", CTX, None),
        P("dp", CTX, None),
        P(),
        P(),
        P(None, None, CTX),
        P(None, None, CTX),
        P("dp", CTX),
        P("dp", CTX, None),
    )
    return jax.shard_map(
        on_device,
        mesh=finer,
        in_specs=placed,
        out_specs=(P(None, ("role", "dp"), CTX), P("role", "dp", CTX, None)),
        check_vma=False,
    )
```

profile of v0, /device:TPU:24, one launch (start us, length us, event | category | flops | bytes accessed | tf_op | source)
XLA Modules:
  0.0 725.8 jit_solution(15006021371325651114)
XLA Ops:
  10.4 16.0 %all_gather.40 = bf16[128,3584]{1,0:T(8,128)(2,1)} all-gather(bf16[32,3584]{1,0:T(8,128)(2,1)S(1)} %get-tuple-element.260), channel_id=1, replica_groups=mesh['role'=2,'dp'=4,'ctx_0'=4,'ctx_1'=4] {'ctx_1'}, dimensions={0}, use_global_device_ids=true | all-gather | bytes 1146880 | tf_op jit(solution)/shard_map/all_gather | solution.py:76
  26.5 16.6 %all_gather.48 = bf16[128,3584]{1,0:T(8,128)(2,1)} all-gather(bf16[32,3584]{1,0:T(8,128)(2,1)S(1)} %get-tuple-element.259), channel_id=1, replica_groups=mesh['role'=2,'dp'=4,'ctx_0'=4,'ctx_1'=4] {'ctx_1'}, dimensions={0}, use_global_device_ids=true | all-gather | bytes 1146880 | tf_op jit(solution)/shard_map/all_gather | solution.py:76
  43.2 14.9 %all_gather.46 = bf16[128,3584]{1,0:T(8,128)(2,1)} all-gather(bf16[32,3584]{1,0:T(8,128)(2,1)S(1)} %get-tuple-element.258), channel_id=1, replica_groups=mesh['role'=2,'dp'=4,'ctx_0'=4,'ctx_1'=4] {'ctx_1'}, dimensions={0}, use_global_device_ids=true | all-gather | bytes 1146880 | tf_op jit(solution)/shard_map/all_gather | solution.py:76
  58.2 14.3 %all_gather.50 = bf16[128,3584]{1,0:T(8,128)(2,1)} all-gather(bf16[32,3584]{1,0:T(8,128)(2,1)S(1)} %get-tuple-element.257), channel_id=1, replica_groups=mesh['role'=2,'dp'=4,'ctx_0'=4,'ctx_1'=4] {'ctx_1'}, dimensions={0}, use_global_device_ids=true | all-gather | bytes 1146880 | tf_op jit(solution)/shard_map/all_gather | solution.py:76
  76.5 23.9 %all_gather.39 = s32[1,2048,5]{1,2,0:T(8,128)S(1)} all-gather(s32[1,128,5]{1,2,0:T(8,128)S(1)} %pad_add_fusion), channel_id=1, replica_groups=mesh['role'=2,'dp'=4,'ctx_0'=4,'ctx_1'=4] {'ctx_0','ctx_1'}, dimensions={1}, use_global_device_ids=true | all-gather | bytes 43520 | tf_op jit(solution)/shard_map/all_gather | solution.py:18
  106.8 11.3 %conditional.12 = (f32[512,4,128]{0,2,1:T(8,128)S(1)}, f32[512,4]{0,1:T(4,128)S(1)}) conditional(s32[]{:T(128)} %convert_element_type.149, (bf16[512,3584]{1,0:T(8,128)(2,1)}, bf16[4,3584,128]{2,1,0:T(8,128)(2,1)}) %tuple.96, () %tuple.97), branch_computations={%region_2.4_spmd, %region_4.0_spmd} | conditional | flops 1879308288 | bytes 16785424 | solution.py:190
  124.1 11.9 %conditional.18 = (f32[512,4,128]{0,2,1:T(8,128)S(1)}, f32[512,4]{0,1:T(4,128)S(1)}) conditional(s32[]{:T(128)} %convert_element_type.149, (bf16[512,3584]{1,0:T(8,128)(2,1)}, bf16[4,3584,128]{2,1,0:T(8,128)(2,1)}) %tuple.108, () %tuple.109), branch_computations={%region_34.36_spmd, %region_36.37_spmd} | conditional | flops 1879308288 | bytes 16785424 | solution.py:190
  136.0 30.0 %all-gather.19.cloned.1.call-done = bf16[512,3584]{1,0:T(8,128)(2,1)} async-done(((bf16[128,3584]{1,0:T(8,128)(2,1)}), bf16[512,3584]{1,0:T(8,128)(2,1)}) %all-gather.19.cloned.1.call-update) | async-done | bytes 3670032 | tf_op jit(solution)/shard_map/all_gather | solution.py:76
  166.0 13.5 %conditional.17 = (f32[512,4,128]{0,2,1:T(8,128)}, f32[512,4]{0,1:T(4,128)S(1)}) conditional(s32[]{:T(128)} %convert_element_type.149, (bf16[512,3584]{1,0:T(8,128)(2,1)}, bf16[4,3584,128]{2,1,0:T(8,128)(2,1)}) %tuple.106, () %tuple.107), branch_computations={%region_28.30_spmd, %region_30.31_spmd} | conditional | flops 1879308288 | bytes 16785424 | solution.py:190
  179.5 32.2 %all-gather.23.cloned.1.call-done = bf16[512,3584]{1,0:T(8,128)(2,1)} async-done(((bf16[128,3584]{1,0:T(8,128)(2,1)}), bf16[512,3584]{1,0:T(8,128)(2,1)}) %all-gather.23.cloned.1.call-update) | async-done | bytes 3670032 | tf_op jit(solution)/shard_map/all_gather | solution.py:76
  211.7 11.7 %conditional.19 = (f32[512,4,128]{0,2,1:T(8,128)S(1)}, f32[512,4]{0,1:T(4,128)S(1)}) conditional(s32[]{:T(128)} %convert_element_type.149, (bf16[512,3584]{1,0:T(8,128)(2,1)}, bf16[4,3584,128]{2,1,0:T(8,128)(2,1)}) %tuple.110, () %tuple.111), branch_computations={%region_40.42_spmd, %region_42.43_spmd} | conditional | flops 1879308288 | bytes 16785424 | solution.py:190
  264.9 11.1 %all-gather.13.cloned.1.call-done = bf16[512,5120]{1,0:T(8,128)(2,1)} async-done(((bf16[32,5120]{1,0:T(8,128)(2,1)}), bf16[512,5120]{1,0:T(8,128)(2,1)}) %all-gather.13.cloned.1.call-update) | async-done | bytes 5242896 | tf_op jit(solution)/shard_map/all_gather | solution.py:164
  277.1 57.0 %all-gather.15.cloned.1.call-done = bf16[512,5120]{1,0:T(8,128)(2,1)} async-done(((bf16[32,5120]{1,0:T(8,128)(2,1)}), bf16[512,5120]{1,0:T(8,128)(2,1)}) %all-gather.15.cloned.1.call-update) | async-done | bytes 5242896 | tf_op jit(solution)/shard_map/all_gather | solution.py:164
  335.3 57.1 %all-gather.17.cloned.1.call-done = bf16[512,5120]{1,0:T(8,128)(2,1)} async-done(((bf16[32,5120]{1,0:T(8,128)(2,1)}), bf16[512,5120]{1,0:T(8,128)(2,1)}) %all-gather.17.cloned.1.call-update) | async-done | bytes 5242896 | tf_op jit(solution)/shard_map/all_gather | solution.py:164
  396.3 54.3 %all-gather.11.cloned.1.call-done = bf16[512,5120]{1,0:T(8,128)(2,1)} async-done(((bf16[32,5120]{1,0:T(8,128)(2,1)}), bf16[512,5120]{1,0:T(8,128)(2,1)}) %all-gather.11.cloned.1.call-update) | async-done | bytes 5242896 | tf_op jit(solution)/shard_map/all_gather | solution.py:164
  460.8 8.5 %all-to-all-done.4 = f32[16,1024,4]{1,2,0:T(4,128)S(1)} async-done(((f32[16,1024,4]{1,2,0:T(4,128)}), f32[16,1024,4]{1,2,0:T(4,128)S(1)}, u32[]{:S(2)}, u32[]{:S(2)}) %all-to-all-start.4) | async-done | bytes 262176 | tf_op jit(solution)/shard_map/all_to_all | solution.py:28
  524.1 46.9 %collective-permute-done = bf16[4,512,4,128]{1,3,2,0:T(8,128)(2,1)} collective-permute-done((bf16[4,512,4,128]{1,3,2,0:T(8,128)(2,1)}, bf16[4,512,4,128]{1,3,2,0:T(8,128)(2,1)}, u32[]{:S(2)}, u32[]{:S(2)}) %collective-permute-start) | collective-permute-done | bytes 2097184 | tf_op jit(solution)/shard_map/ppermute | solution.py:83
  580.8 9.7 %conditional.21 = (f32[4,3584,128]{1,2,0:T(8,128)}) conditional(s32[]{:T(128)} %convert_element_type.149, (bf16[512,4,128]{0,2,1:T(8,128)(2,1)}, bf16[512,3584]{1,0:T(8,128)(2,1)}, f32[4,3584,128]{1,2,0:T(8,128)}) %tuple.114, f32[4,3584,128]{1,2,0:T(8,128)} %get-tuple-element.317), branch_computations={%region_47.48_spmd, %region_48.49_spmd} | conditional | flops 1880883200 | bytes 18874376 | solution.py:233
  581.0 9.5 %bitcast_add_fusion = f32[4,3584,128]{1,2,0:T(8,128)} fusion(f32[4,3584,128]{1,2,0:T(8,128)} %get-tuple-element.107, bf16[512,4,128]{0,2,1:T(8,128)(2,1)} %get-tuple-element.108, bf16[512,3584]{1,0:T(8,128)(2,1)} %get-tuple-element.109), kind=kOutput, calls=%fused_computation.10 | convolution fusion | flops 1880883200 | bytes 18874368 | tf_op jit(solution)/shard_map/cond/branch_0_fun/rd,rqc->qdc/dot_general | solution.py:237
  590.5 9.5 %conditional.22 = (f32[4,3584,128]{1,2,0:T(8,128)}) conditional(s32[]{:T(128)} %convert_element_type.149, (bf16[512,4,128]{0,2,1:T(8,128)(2,1)}, bf16[512,3584]{1,0:T(8,128)(2,1)}, f32[4,3584,128]{1,2,0:T(8,128)}) %tuple.115, f32[4,3584,128]{1,2,0:T(8,128)} %get-tuple-element.318), branch_computations={%region_49.50_spmd, %region_50.51_spmd} | conditional | flops 1880883200 | bytes 18874376 | solution.py:233
  590.5 9.5 %bitcast_add_fusion.1 = f32[4,3584,128]{1,2,0:T(8,128)} fusion(f32[4,3584,128]{1,2,0:T(8,128)} %get-tuple-element.110, bf16[512,4,128]{0,2,1:T(8,128)(2,1)} %get-tuple-element.111, bf16[512,3584]{1,0:T(8,128)(2,1)} %get-tuple-element.112), kind=kOutput, calls=%fused_computation.12 | convolution fusion | flops 1880883200 | bytes 18874368 | tf_op jit(solution)/shard_map/cond/branch_0_fun/rd,rqc->qdc/dot_general | solution.py:237
  601.7 9.4 %conditional.23 = (f32[4,3584,128]{1,2,0:T(8,128)}) conditional(s32[]{:T(128)} %convert_element_type.149, (bf16[512,4,128]{0,2,1:T(8,128)(2,1)S(1)}, bf16[512,3584]{1,0:T(8,128)(2,1)}, f32[4,3584,128]{1,2,0:T(8,128)}) %tuple.116, f32[4,3584,128]{1,2,0:T(8,128)} %get-tuple-element.319), branch_computations={%region_51.52_spmd, %region_52.53_spmd} | conditional | flops 1880883200 | bytes 18874376 | solution.py:233
  601.7 9.4 %bitcast_add_fusion.2 = f32[4,3584,128]{1,2,0:T(8,128)} fusion(f32[4,3584,128]{1,2,0:T(8,128)} %get-tuple-element.113, bf16[512,4,128]{0,2,1:T(8,128)(2,1)S(1)} %get-tuple-element.114, bf16[512,3584]{1,0:T(8,128)(2,1)} %get-tuple-element.115), kind=kOutput, calls=%fused_computation.14 | convolution fusion | flops 1880883200 | bytes 18874368 | tf_op jit(solution)/shard_map/cond/branch_0_fun/rd,rqc->qdc/dot_general | solution.py:237
  611.1 8.4 %copy.52 = f32[4,3584,128]{2,1,0:T(8,128)} copy(f32[4,3584,128]{1,2,0:T(8,128)} %get-tuple-element.320) | data formatting | bytes 14680064 | tf_op jit(solution)/shard_map/cond | solution.py:233
  (333 shorter events, 297.9 us)
Async XLA Ops:
  7.2 99.6 %all-gather.9.cloned.1.call-start = ((), (), s32[]{:S(2)}) async-start(), calls=%async_computation.17 | async-start | bytes 4587520 | tf_op jit(solution)/shard_map/all_gather | solution.py:76
  26.4 97.7 %all-gather.21.cloned.1.call-start = ((), (), s32[]{:S(2)}) async-start(), calls=%async_computation.23 | async-start | bytes 4587520 | tf_op jit(solution)/shard_map/all_gather | solution.py:76
  43.1 122.9 %all-gather.19.cloned.1.call-start = ((), (), s32[]{:S(2)}) async-start(), calls=%async_computation.22 | async-start | bytes 4587520 | tf_op jit(solution)/shard_map/all_gather | solution.py:76
  58.1 153.6 %all-gather.23.cloned.1.call-start = ((), (), s32[]{:S(2)}) async-start(), calls=%async_computation.24 | async-start | bytes 4587520 | tf_op jit(solution)/shard_map/all_gather | solution.py:76
  72.5 203.5 %all-gather.13.cloned.1.call-start = ((), (), s32[]{:S(2)}) async-start(), calls=%async_computation.19 | async-start | bytes 5570560 | tf_op jit(solution)/shard_map/all_gather | solution.py:164
  74.4 259.7 %all-gather.15.cloned.1.call-start = ((), (), s32[]{:S(2)}) async-start(), calls=%async_computation.20 | async-start | bytes 5570560 | tf_op jit(solution)/shard_map/all_gather | solution.py:164
  75.0 317.4 %all-gather.17.cloned.1.call-start = ((), (), s32[]{:S(2)}) async-start(), calls=%async_computation.21 | async-start | bytes 5570560 | tf_op jit(solution)/shard_map/all_gather | solution.py:164
  75.7 374.9 %all-gather.11.cloned.1.call-start = ((), (), s32[]{:S(2)}) async-start(), calls=%async_computation.18 | async-start | bytes 5570560 | tf_op jit(solution)/shard_map/all_gather | solution.py:164
  119.2 108.2 %all-to-all-start = ((f32[16,1536,4]{1,2,0:T(4,128)}), f32[16,1536,4]{1,2,0:T(4,128)S(1)}, u32[]{:S(2)}, u32[]{:S(2)}) async-start(f32[16,1536,4]{1,2,0:T(4,128)} %broadcast_in_dim.25), calls=%async_computation | async-start | bytes 786432 | tf_op jit(solution)/shard_map/all_to_all | solution.py:28
  229.0 15.9 %all-to-all-start.7 = ((f32[16,1536,4]{1,2,0:T(4,128)}), f32[16,1536,4]{1,2,0:T(4,128)}, u32[]{:S(2)}, u32[]{:S(2)}) async-start(f32[16,1536,4]{1,2,0:T(4,128)} %broadcast_in_dim.32), calls=%async_computation.7 | async-start | bytes 786432 | tf_op jit(solution)/shard_map/all_to_all | solution.py:28
  246.4 17.0 %all-to-all-start.6 = ((f32[16,1536,4]{1,2,0:T(4,128)}), f32[16,1536,4]{1,2,0:T(4,128)S(1)}, u32[]{:S(2)}, u32[]{:S(2)}) async-start(f32[16,1536,4]{1,2,0:T(4,128)} %broadcast_in_dim.31), calls=%async_computation.6 | async-start | bytes 786432 | tf_op jit(solution)/shard_map/all_to_all | solution.py:28
  455.5 13.8 %all-to-all-start.4 = ((f32[16,1024,4]{1,2,0:T(4,128)}), f32[16,1024,4]{1,2,0:T(4,128)S(1)}, u32[]{:S(2)}, u32[]{:S(2)}) async-start(f32[16,1024,4]{1,2,0:T(4,128)} %broadcast_in_dim.29), calls=%async_computation.4 | async-start | bytes 524288 | tf_op jit(solution)/shard_map/all_to_all | solution.py:28
  470.1 12.2 %all-to-all-start.3 = ((f32[16,1024,4]{1,2,0:T(4,128)}), f32[16,1024,4]{1,2,0:T(4,128)S(1)}, u32[]{:S(2)}, u32[]{:S(2)}) async-start(f32[16,1024,4]{1,2,0:T(4,128)} %broadcast_in_dim.28), calls=%async_computation.3 | async-start | bytes 524288 | tf_op jit(solution)/shard_map/all_to_all | solution.py:28
  483.1 12.1 %all-to-all-start.2 = ((f32[16,1024,4]{1,2,0:T(4,128)}), f32[16,1024,4]{1,2,0:T(4,128)S(1)}, u32[]{:S(2)}, u32[]{:S(2)}) async-start(f32[16,1024,4]{1,2,0:T(4,128)} %broadcast_in_dim.27), calls=%async_computation.2 | async-start | bytes 524288 | tf_op jit(solution)/shard_map/all_to_all | solution.py:28
  496.1 12.1 %all-to-all-start.1 = ((f32[16,1024,4]{1,2,0:T(4,128)}), f32[16,1024,4]{1,2,0:T(4,128)S(1)}, u32[]{:S(2)}, u32[]{:S(2)}) async-start(f32[16,1024,4]{1,2,0:T(4,128)} %broadcast_in_dim.26), calls=%async_computation.1 | async-start | bytes 524288 | tf_op jit(solution)/shard_map/all_to_all | solution.py:28
  509.1 14.7 %all-to-all-start.5 = ((f32[16,1536,4]{1,2,0:T(4,128)}), f32[16,1536,4]{1,2,0:T(4,128)S(1)}, u32[]{:S(2)}, u32[]{:S(2)}) async-start(f32[16,1536,4]{1,2,0:T(4,128)} %broadcast_in_dim.30), calls=%async_computation.5 | async-start | bytes 786432 | tf_op jit(solution)/shard_map/all_to_all | solution.py:28
  514.6 204.4 %reduce-scatter.2.cloned.1.call-start = ((), (), s32[]{:S(2)}) async-start(), calls=%async_computation.25 | async-start | bytes 8257536 | tf_op jit(solution)/shard_map/reduce_scatter | solution.py:244
  519.9 51.2 %collective-permute-start = (bf16[4,512,4,128]{1,3,2,0:T(8,128)(2,1)}, bf16[4,512,4,128]{1,3,2,0:T(8,128)(2,1)}, u32[]{:S(2)}, u32[]{:S(2)}) collective-permute-start(bf16[4,512,4,128]{1,3,2,0:T(8,128)(2,1)} %pad_maximum_fusion), channel_id=1, source_target_pairs={{0,64},{1,65},{2,66},{3,67},{4,68},{5,69},{6,70},{7,71},{8,72},{9,... | collective-permute-start | bytes 6291464 | tf_op jit(solution)/shard_map/ppermute | solution.py:83
  621.0 14.5 %all-to-all-start.14 = ((f32[16,1,128]{2,1,0:T(1,128)}), f32[16,1,128]{2,1,0:T(1,128)S(1)}, u32[]{:S(2)}, u32[]{:S(2)}) async-start(f32[16,1,128]{2,1,0:T(1,128)} %reshape.455), calls=%async_computation.15 | async-start | bytes 16384 | tf_op jit(solution)/shard_map/all_to_all | solution.py:69
  635.5 10.9 %all-to-all-start.12 = ((f32[16,1,128]{2,1,0:T(1,128)}), f32[16,1,128]{2,1,0:T(1,128)S(1)}, u32[]{:S(2)}, u32[]{:S(2)}) async-start(f32[16,1,128]{2,1,0:T(1,128)} %reshape.459), calls=%async_computation.13 | async-start | bytes 16384 | tf_op jit(solution)/shard_map/all_to_all | solution.py:69
  657.3 10.9 %all-to-all-start.8 = ((f32[16,1,128]{2,1,0:T(1,128)}), f32[16,1,128]{2,1,0:T(1,128)S(1)}, u32[]{:S(2)}, u32[]{:S(2)}) async-start(f32[16,1,128]{2,1,0:T(1,128)} %reshape.467), calls=%async_computation.9 | async-start | bytes 16384 | tf_op jit(solution)/shard_map/all_to_all | solution.py:69
  673.7 11.0 %all-to-all-start.15 = ((f32[16,1,128]{2,1,0:T(1,128)}), f32[16,1,128]{2,1,0:T(1,128)S(1)}, u32[]{:S(2)}, u32[]{:S(2)}) async-start(f32[16,1,128]{2,1,0:T(1,128)} %reshape.457), calls=%async_computation.16 | async-start | bytes 16384 | tf_op jit(solution)/shard_map/all_to_all | solution.py:69
  684.7 10.9 %all-to-all-start.13 = ((f32[16,1,128]{2,1,0:T(1,128)}), f32[16,1,128]{2,1,0:T(1,128)S(1)}, u32[]{:S(2)}, u32[]{:S(2)}) async-start(f32[16,1,128]{2,1,0:T(1,128)} %reshape.461), calls=%async_computation.14 | async-start | bytes 16384 | tf_op jit(solution)/shard_map/all_to_all | solution.py:69
  695.6 11.0 %all-to-all-start.11 = ((f32[16,1,128]{2,1,0:T(1,128)}), f32[16,1,128]{2,1,0:T(1,128)S(1)}, u32[]{:S(2)}, u32[]{:S(2)}) async-start(f32[16,1,128]{2,1,0:T(1,128)} %reshape.465), calls=%async_computation.12 | async-start | bytes 16384 | tf_op jit(solution)/shard_map/all_to_all | solution.py:69
  (42 other events, 664.2 us)
Sparse Core Ops, SparseCore 0:
  26.5 45.5 all-gather.8
  73.8 46.2 all-gather.20
  121.8 44.1 all-gather.18
  167.5 44.1 all-gather.22
  213.7 62.2 all-gather.12
  278.0 56.0 all-gather.14
  336.3 56.0 all-gather.16
  394.6 56.0 all-gather.10
  619.7 46.5 reduce-scatter.1
where the time goes:
time: 736 us; the launch traced here: 726 us
  waiting for transfers between devices  378 us (51%)
  blocking collectives  85.7 us (12%)
  starting transfers between devices  69.3 us (9%)
  local copies, waits for them, and re-layouts  65.5 us (9%)
  matrix products  56.1 us (8%)
  other arithmetic  54.6 us (7%)
  between operations  15.2 us (2%)
    all_gather x4, waiting for transfers between devices, on_device(): lax.all_gather(teacher_local_rows, CTX, axis=0, tiled=True)  180 us
    all_gather x4, waiting for transfers between devices, whole_of(): filled = lax.all_gather(filled, axes[number], axis=dim, tiled=True)  62.2 us
    all_gather x4, blocking collectives, whole_of(): filled = lax.all_gather(filled, axes[number], axis=dim, tiled=True)  61.8 us
    all_to_all x8, waiting for transfers between devices, sum_at_owner(): lax.all_to_all(cut_along(array, dim, length), axis, 0, 0, tiled=True)  49.9 us
    ppermute x1, waiting for transfers between devices, shifted(): lax.ppermute(value, axis, [(source, source + steps) for source in range(i...  46.9 us
    all_to_all x8, waiting for transfers between devices, copy_for_each(): return lax.all_to_all(copies, axis, split_axis=0, concat_axis=0, tiled=True)  37.9 us
    all_to_all x8, starting transfers between devices, copy_for_each(): return lax.all_to_all(copies, axis, split_axis=0, concat_axis=0, tiled=True)  36.6 us
    dot_general x4, matrix products, on_device(): jnp.einsum('rd,rqc->qdc', gathered, gradient_scaling, preferred_element_t...  33.5 us
  transfers between devices with their start and end apart: 26, of which 22 were waited for; matrix products, arithmetic and copies ran while one was open for 16% of the time, Pallas kernels for 0%

commit v1 on v0

--- a/solution.py
+++ b/solution.py
@@ -1,3 +1,4 @@
+import functools
 import jax
 import jax.numpy as jnp
 from jax import lax
@@ -10,6 +11,18 @@
 epsilon = 1e-06
 sharpness_divisor = 2.0
 blend_ratio = 0.5
+
+
+def try_all_shifts_all_on_mesh(xs, row_dim):
+    return jnp.concatenate(
+        lax.all_to_all(
+            jnp.stack(lax.psum(1, CTX) * [xs], axis=0), axis_name=CTX, split_axis=0, concat_axis=0
+        ),
+        axis=row_dim,
+    )
+
+
+_see_packet = functools.partial(try_all_shifts_all_on_mesh, row_dim=0)
 
 
 def sent_together(arrays, axis, dim, along):
@@ -161,7 +174,7 @@
                     "rd,qdc->rqc", piece, mentor_output_weights, preferred_element_type=jnp.float32
                 ),
                 lambda piece: jnp.zeros((piece.shape[0], QUANTIZER_TOTAL, columns), jnp.float32),
-                lax.all_gather(teacher_local_rows, CTX, axis=0, tiled=True),
+                _see_packet(teacher_local_rows),
             )
             / sharpness_divisor
         )

time: 736 us -> 817 us (1.11)
  blocking collectives: 85.7 us -> 273 us
  waiting for transfers between devices: 378 us -> 250 us
  starting transfers between devices: 69.3 us -> 104 us
  other arithmetic: 54.6 us -> 39.7 us
    all_gather x4 -> x0, waiting for transfers between devices: 180 us -> none  [on_device(): lax.all_gather(teacher_local_rows, CTX, axis=0, tiled=True)]
    all_gather x4, blocking collectives: 61.8 us -> 193 us  [whole_of(): filled = lax.all_gather(filled, axes[number], axis=dim, tiled=True)]
    all_to_all x0 -> x4, waiting for transfers between devices: none -> 120 us  [try_all_shifts_all_on_mesh(): lax.all_to_all(jnp.stack(lax.psum(1, CTX) * [xs], axis=0), axis_name=CTX,...]
    all_gather x4, waiting for transfers between devices: 62.2 us -> 0.04 us  [whole_of(): filled = lax.all_gather(filled, axes[number], axis=dim, tiled=True)]
    all_gather x1, blocking collectives: 23.9 us -> 79.5 us  [sent_together(): filled, at, done = (lax.all_gather(both, axis, axis=dim, tiled=True), 0, [])]
    all_to_all x0 -> x4, starting transfers between devices: none -> 38.1 us  [try_all_shifts_all_on_mesh(): lax.all_to_all(jnp.stack(lax.psum(1, CTX) * [xs], axis=0), axis_name=CTX,...]
    ppermute x1, waiting for transfers between devices: 46.9 us -> 32.9 us  [shifted(): lax.ppermute(value, axis, [(source, source + steps) for source in range(i...]
    another operation x8 -> x12, local copies, waits for them, and re-layouts: 26.3 us -> 36.2 us
  transfers between devices with their start and end apart: 26 -> 26, of which waited for: 22 -> 19; matrix products, arithmetic and copies ran while one was open for 16% -> 13% of each run, Pallas kernels for 0% -> 0%
where the time goes in v1:
time: 817 us; the launch traced here: 807 us
  blocking collectives  273 us (33%)
  waiting for transfers between devices  250 us (31%)
  starting transfers between devices  104 us (13%)
  local copies, waits for them, and re-layouts  69.4 us (8%)
  matrix products  54.6 us (7%)
  other arithmetic  39.7 us (5%)
  between operations  15.3 us (2%)
    all_gather x4, blocking collectives, whole_of(): filled = lax.all_gather(filled, axes[number], axis=dim, tiled=True)  193 us
    all_to_all x4, waiting for transfers between devices, try_all_shifts_all_on_mesh(): lax.all_to_all(jnp.stack(lax.psum(1, CTX) * [xs], axis=0), axis_name=CTX,...  120 us
    all_gather x1, blocking collectives, sent_together(): filled, at, done = (lax.all_gather(both, axis, axis=dim, tiled=True), 0, [])  79.5 us
    all_to_all x8, waiting for transfers between devices, sum_at_owner(): lax.all_to_all(cut_along(array, dim, length), axis, 0, 0, tiled=True)  51.6 us
    all_to_all x8, waiting for transfers between devices, copy_for_each(): return lax.all_to_all(copies, axis, split_axis=0, concat_axis=0, tiled=True)  45.4 us
    all_to_all x4, starting transfers between devices, try_all_shifts_all_on_mesh(): lax.all_to_all(jnp.stack(lax.psum(1, CTX) * [xs], axis=0), axis_name=CTX,...  38.1 us
    dot_general x4, matrix products, on_device(): jnp.einsum('rd,rqc->qdc', gathered, gradient_scaling, preferred_element_t...  33.5 us
    all_to_all x8, starting transfers between devices, copy_for_each(): return lax.all_to_all(copies, axis, split_axis=0, concat_axis=0, tiled=True)  33.3 us
  transfers between devices with their start and end apart: 26, of which 19 were waited for; matrix products, arithmetic and copies ran while one was open for 13% of the time, Pallas kernels for 0%

profile of v1, /device:TPU:24, one launch (start us, length us, event | category | flops | bytes accessed | tf_op | source)
XLA Modules:
  0.0 806.8 jit_solution(10987410289568129229)
XLA Ops:
  22.3 67.1 %all_gather.28 = bf16[128,3584]{1,0:T(8,128)(2,1)} all-gather(bf16[32,3584]{1,0:T(8,128)(2,1)S(1)} %get-tuple-element.264), channel_id=1, replica_groups=mesh['role'=2,'dp'=4,'ctx_0'=4,'ctx_1'=4] {'ctx_1'}, dimensions={0}, use_global_device_ids=true | all-gather | bytes 1146880 | tf_op jit(solution)/shard_map/all_gather | solution.py:89
  89.4 11.2 %all-to-all-done.1 = bf16[16,32,5120]{2,1,0:T(8,128)(2,1)} async-done(((bf16[16,32,5120]{2,1,0:T(8,128)(2,1)}), bf16[16,32,5120]{2,1,0:T(8,128)(2,1)}, u32[]{:S(2)}, u32[]{:S(2)}) %all-to-all-start.1) | async-done | bytes 5242912 | tf_op jit(solution)/shard_map/all_to_all | solution.py:18
  103.6 12.3 %all-to-all-start.3 = ((bf16[16,32,5120]{2,1,0:T(8,128)(2,1)}), bf16[16,32,5120]{2,1,0:T(8,128)(2,1)}, u32[]{:S(2)}, u32[]{:S(2)}) async-start(bf16[16,32,5120]{2,1,0:T(8,128)(2,1)} %stack.30), calls=%async_computation.3 | async-start | bytes 10485760 | tf_op jit(solution)/shard_map/all_to_all | solution.py:18
  116.0 42.6 %all_gather.32 = bf16[128,3584]{1,0:T(8,128)(2,1)} all-gather(bf16[32,3584]{1,0:T(8,128)(2,1)S(1)} %get-tuple-element.263), channel_id=1, replica_groups=mesh['role'=2,'dp'=4,'ctx_0'=4,'ctx_1'=4] {'ctx_1'}, dimensions={0}, use_global_device_ids=true | all-gather | bytes 1146880 | tf_op jit(solution)/shard_map/all_gather | solution.py:89
  158.6 48.9 %all-to-all-done.3 = bf16[16,32,5120]{2,1,0:T(8,128)(2,1)} async-done(((bf16[16,32,5120]{2,1,0:T(8,128)(2,1)}), bf16[16,32,5120]{2,1,0:T(8,128)(2,1)}, u32[]{:S(2)}, u32[]{:S(2)}) %all-to-all-start.3) | async-done | bytes 5242912 | tf_op jit(solution)/shard_map/all_to_all | solution.py:18
  210.4 10.0 %all-to-all-start.5 = ((bf16[16,32,5120]{2,1,0:T(8,128)(2,1)}), bf16[16,32,5120]{2,1,0:T(8,128)(2,1)}, u32[]{:S(2)}, u32[]{:S(2)}) async-start(bf16[16,32,5120]{2,1,0:T(8,128)(2,1)} %stack.33), calls=%async_computation.5 | async-start | bytes 10485760 | tf_op jit(solution)/shard_map/all_to_all | solution.py:18
  220.5 41.6 %all_gather.30 = bf16[128,3584]{1,0:T(8,128)(2,1)} all-gather(bf16[32,3584]{1,0:T(8,128)(2,1)S(1)} %get-tuple-element.262), channel_id=1, replica_groups=mesh['role'=2,'dp'=4,'ctx_0'=4,'ctx_1'=4] {'ctx_1'}, dimensions={0}, use_global_device_ids=true | all-gather | bytes 1146880 | tf_op jit(solution)/shard_map/all_gather | solution.py:89
  262.2 59.9 %all-to-all-done.5 = bf16[16,32,5120]{2,1,0:T(8,128)(2,1)} async-done(((bf16[16,32,5120]{2,1,0:T(8,128)(2,1)}), bf16[16,32,5120]{2,1,0:T(8,128)(2,1)}, u32[]{:S(2)}, u32[]{:S(2)}) %all-to-all-start.5) | async-done | bytes 5242912 | tf_op jit(solution)/shard_map/all_to_all | solution.py:18
  332.7 42.2 %all_gather.34 = bf16[128,3584]{1,0:T(8,128)(2,1)} all-gather(bf16[32,3584]{1,0:T(8,128)(2,1)S(1)} %get-tuple-element.261), channel_id=1, replica_groups=mesh['role'=2,'dp'=4,'ctx_0'=4,'ctx_1'=4] {'ctx_1'}, dimensions={0}, use_global_device_ids=true | all-gather | bytes 1146880 | tf_op jit(solution)/shard_map/all_gather | solution.py:89
  374.9 79.5 %all_gather.27 = s32[1,2048,5]{1,2,0:T(8,128)S(1)} all-gather(s32[1,128,5]{1,2,0:T(8,128)S(1)} %pad_add_fusion), channel_id=1, replica_groups=mesh['role'=2,'dp'=4,'ctx_0'=4,'ctx_1'=4] {'ctx_0','ctx_1'}, dimensions={1}, use_global_device_ids=true | all-gather | bytes 43520 | tf_op jit(solution)/shard_map/all_gather | solution.py:31
  479.0 8.4 %all-to-all-done.6 = f32[16,1024,4]{1,2,0:T(4,128)} async-done(((f32[16,1024,4]{1,2,0:T(4,128)}), f32[16,1024,4]{1,2,0:T(4,128)}, u32[]{:S(2)}, u32[]{:S(2)}) %all-to-all-start.6) | async-done | bytes 262176 | tf_op jit(solution)/shard_map/all_to_all | solution.py:41
  514.0 11.3 %conditional.12 = (f32[512,4,128]{0,2,1:T(8,128)S(1)}, f32[512,4]{0,1:T(4,128)S(1)}) conditional(s32[]{:T(128)} %convert_element_type.149, (bf16[512,3584]{1,0:T(8,128)(2,1)}, bf16[4,3584,128]{2,1,0:T(8,128)(2,1)}) %tuple.96, () %tuple.97), branch_computations={%region_2.4_spmd, %region_4.0_spmd} | conditional | flops 1879308288 | bytes 16785424 | solution.py:203
  530.1 11.3 %conditional.18 = (f32[512,4,128]{0,2,1:T(8,128)S(1)}, f32[512,4]{0,1:T(4,128)S(1)}) conditional(s32[]{:T(128)} %convert_element_type.149, (bf16[512,3584]{1,0:T(8,128)(2,1)}, bf16[4,3584,128]{2,1,0:T(8,128)(2,1)}) %tuple.108, () %tuple.109), branch_computations={%region_34.36_spmd, %region_36.37_spmd} | conditional | flops 1879308288 | bytes 16785424 | solution.py:203
  541.5 11.5 %conditional.17 = (f32[512,4,128]{0,2,1:T(8,128)S(1)}, f32[512,4]{0,1:T(4,128)S(1)}) conditional(s32[]{:T(128)} %convert_element_type.149, (bf16[512,3584]{1,0:T(8,128)(2,1)}, bf16[4,3584,128]{2,1,0:T(8,128)(2,1)}) %tuple.106, () %tuple.107), branch_computations={%region_28.30_spmd, %region_30.31_spmd} | conditional | flops 1879308288 | bytes 16785424 | solution.py:203
  554.9 11.3 %conditional.19 = (f32[512,4,128]{0,2,1:T(8,128)S(1)}, f32[512,4]{0,1:T(4,128)S(1)}) conditional(s32[]{:T(128)} %convert_element_type.149, (bf16[512,3584]{1,0:T(8,128)(2,1)}, bf16[4,3584,128]{2,1,0:T(8,128)(2,1)}) %tuple.110, () %tuple.111), branch_computations={%region_40.42_spmd, %region_42.43_spmd} | conditional | flops 1879308288 | bytes 16785424 | solution.py:203
  577.4 10.0 %all-to-all-done.10 = f32[16,1536,4]{1,2,0:T(4,128)} async-done(((f32[16,1536,4]{1,2,0:T(4,128)}), f32[16,1536,4]{1,2,0:T(4,128)}, u32[]{:S(2)}, u32[]{:S(2)}) %all-to-all-start.10) | async-done | bytes 393248 | tf_op jit(solution)/shard_map/all_to_all | solution.py:41
  617.6 32.9 %collective-permute-done = bf16[4,512,4,128]{1,3,2,0:T(8,128)(2,1)} collective-permute-done((bf16[4,512,4,128]{1,3,2,0:T(8,128)(2,1)}, bf16[4,512,4,128]{1,3,2,0:T(8,128)(2,1)}, u32[]{:S(2)}, u32[]{:S(2)}) %collective-permute-start) | collective-permute-done | bytes 2097184 | tf_op jit(solution)/shard_map/ppermute | solution.py:96
  660.2 9.7 %conditional.21 = (f32[4,3584,128]{1,2,0:T(8,128)}) conditional(s32[]{:T(128)} %convert_element_type.149, (bf16[512,4,128]{0,2,1:T(8,128)(2,1)}, bf16[512,3584]{1,0:T(8,128)(2,1)}, f32[4,3584,128]{1,2,0:T(8,128)}) %tuple.114, f32[4,3584,128]{1,2,0:T(8,128)} %get-tuple-element.321), branch_computations={%region_47.48_spmd, %region_48.49_spmd} | conditional | flops 1880883200 | bytes 18874376 | solution.py:246
  660.4 9.5 %bitcast_add_fusion = f32[4,3584,128]{1,2,0:T(8,128)} fusion(f32[4,3584,128]{1,2,0:T(8,128)} %get-tuple-element.111, bf16[512,4,128]{0,2,1:T(8,128)(2,1)} %get-tuple-element.112, bf16[512,3584]{1,0:T(8,128)(2,1)} %get-tuple-element.113), kind=kOutput, calls=%fused_computation.2 | convolution fusion | flops 1880883200 | bytes 18874368 | tf_op jit(solution)/shard_map/cond/branch_0_fun/rd,rqc->qdc/dot_general | solution.py:250
  669.9 9.5 %conditional.22 = (f32[4,3584,128]{1,2,0:T(8,128)}) conditional(s32[]{:T(128)} %convert_element_type.149, (bf16[512,4,128]{0,2,1:T(8,128)(2,1)}, bf16[512,3584]{1,0:T(8,128)(2,1)}, f32[4,3584,128]{1,2,0:T(8,128)}) %tuple.115, f32[4,3584,128]{1,2,0:T(8,128)} %get-tuple-element.322), branch_computations={%region_49.50_spmd, %region_50.51_spmd} | conditional | flops 1880883200 | bytes 18874376 | solution.py:246
  669.9 9.5 %bitcast_add_fusion.1 = f32[4,3584,128]{1,2,0:T(8,128)} fusion(f32[4,3584,128]{1,2,0:T(8,128)} %get-tuple-element.114, bf16[512,4,128]{0,2,1:T(8,128)(2,1)} %get-tuple-element.115, bf16[512,3584]{1,0:T(8,128)(2,1)} %get-tuple-element.116), kind=kOutput, calls=%fused_computation.4 | convolution fusion | flops 1880883200 | bytes 18874368 | tf_op jit(solution)/shard_map/cond/branch_0_fun/rd,rqc->qdc/dot_general | solution.py:250
  681.1 9.4 %conditional.23 = (f32[4,3584,128]{1,2,0:T(8,128)}) conditional(s32[]{:T(128)} %convert_element_type.149, (bf16[512,4,128]{0,2,1:T(8,128)(2,1)S(1)}, bf16[512,3584]{1,0:T(8,128)(2,1)}, f32[4,3584,128]{1,2,0:T(8,128)}) %tuple.116, f32[4,3584,128]{1,2,0:T(8,128)} %get-tuple-element.323), branch_computations={%region_51.52_spmd, %region_52.53_spmd} | conditional | flops 1880883200 | bytes 18874376 | solution.py:246
  681.1 9.4 %bitcast_add_fusion.2 = f32[4,3584,128]{1,2,0:T(8,128)} fusion(f32[4,3584,128]{1,2,0:T(8,128)} %get-tuple-element.117, bf16[512,4,128]{0,2,1:T(8,128)(2,1)S(1)} %get-tuple-element.118, bf16[512,3584]{1,0:T(8,128)(2,1)} %get-tuple-element.119), kind=kOutput, calls=%fused_computation.6 | convolution fusion | flops 1880883200 | bytes 18874368 | tf_op jit(solution)/shard_map/cond/branch_0_fun/rd,rqc->qdc/dot_general | solution.py:250
  690.5 8.4 %copy.52 = f32[4,3584,128]{2,1,0:T(8,128)} copy(f32[4,3584,128]{1,2,0:T(8,128)} %get-tuple-element.324) | data formatting | bytes 14680064 | tf_op jit(solution)/shard_map/cond | solution.py:246
  (325 shorter events, 293.3 us)
Async XLA Ops:
  13.5 87.1 %all-to-all-start.1 = ((bf16[16,32,5120]{2,1,0:T(8,128)(2,1)}), bf16[16,32,5120]{2,1,0:T(8,128)(2,1)}, u32[]{:S(2)}, u32[]{:S(2)}) async-start(bf16[16,32,5120]{2,1,0:T(8,128)(2,1)} %stack.27), calls=%async_computation.1 | async-start | bytes 10485760 | tf_op jit(solution)/shard_map/all_to_all | solution.py:18
  21.6 492.4 %all-gather.5.cloned.1.call-start = ((), (), s32[]{:S(2)}) async-start(), calls=%async_computation.21 | async-start | bytes 4587520 | tf_op jit(solution)/shard_map/all_gather | solution.py:89
  103.6 103.9 %all-to-all-start.3 = ((bf16[16,32,5120]{2,1,0:T(8,128)(2,1)}), bf16[16,32,5120]{2,1,0:T(8,128)(2,1)}, u32[]{:S(2)}, u32[]{:S(2)}) async-start(bf16[16,32,5120]{2,1,0:T(8,128)(2,1)} %stack.30), calls=%async_computation.3 | async-start | bytes 10485760 | tf_op jit(solution)/shard_map/all_to_all | solution.py:18
  116.0 414.2 %all-gather.9.cloned.1.call-start = ((), (), s32[]{:S(2)}) async-start(), calls=%async_computation.23 | async-start | bytes 4587520 | tf_op jit(solution)/shard_map/all_gather | solution.py:89
  210.4 111.6 %all-to-all-start.5 = ((bf16[16,32,5120]{2,1,0:T(8,128)(2,1)}), bf16[16,32,5120]{2,1,0:T(8,128)(2,1)}, u32[]{:S(2)}, u32[]{:S(2)}) async-start(bf16[16,32,5120]{2,1,0:T(8,128)(2,1)} %stack.33), calls=%async_computation.5 | async-start | bytes 10485760 | tf_op jit(solution)/shard_map/all_to_all | solution.py:18
  220.5 321.0 %all-gather.7.cloned.1.call-start = ((), (), s32[]{:S(2)}) async-start(), calls=%async_computation.22 | async-start | bytes 4587520 | tf_op jit(solution)/shard_map/all_gather | solution.py:89
  325.0 135.9 %all-to-all-start.7 = ((bf16[16,32,5120]{2,1,0:T(8,128)(2,1)}), bf16[16,32,5120]{2,1,0:T(8,128)(2,1)}, u32[]{:S(2)}, u32[]{:S(2)}) async-start(bf16[16,32,5120]{2,1,0:T(8,128)(2,1)} %stack.36), calls=%async_computation.7 | async-start | bytes 10485760 | tf_op jit(solution)/shard_map/all_to_all | solution.py:18
  332.6 222.3 %all-gather.11.cloned.1.call-start = ((), (), s32[]{:S(2)}) async-start(), calls=%async_computation.24 | async-start | bytes 4587520 | tf_op jit(solution)/shard_map/all_gather | solution.py:89
  461.7 12.2 %all-to-all-start.4 = ((f32[16,1024,4]{1,2,0:T(4,128)}), f32[16,1024,4]{1,2,0:T(4,128)S(1)}, u32[]{:S(2)}, u32[]{:S(2)}) async-start(f32[16,1024,4]{1,2,0:T(4,128)} %broadcast_in_dim.27), calls=%async_computation.4 | async-start | bytes 524288 | tf_op jit(solution)/shard_map/all_to_all | solution.py:41
  474.7 12.8 %all-to-all-start.6 = ((f32[16,1024,4]{1,2,0:T(4,128)}), f32[16,1024,4]{1,2,0:T(4,128)}, u32[]{:S(2)}, u32[]{:S(2)}) async-start(f32[16,1024,4]{1,2,0:T(4,128)} %broadcast_in_dim.28), calls=%async_computation.6 | async-start | bytes 524288 | tf_op jit(solution)/shard_map/all_to_all | solution.py:41
  488.2 12.2 %all-to-all-start.8 = ((f32[16,1024,4]{1,2,0:T(4,128)}), f32[16,1024,4]{1,2,0:T(4,128)S(1)}, u32[]{:S(2)}, u32[]{:S(2)}) async-start(f32[16,1024,4]{1,2,0:T(4,128)} %broadcast_in_dim.29), calls=%async_computation.8 | async-start | bytes 524288 | tf_op jit(solution)/shard_map/all_to_all | solution.py:41
  501.1 12.0 %all-to-all-start.2 = ((f32[16,1024,4]{1,2,0:T(4,128)}), f32[16,1024,4]{1,2,0:T(4,128)S(1)}, u32[]{:S(2)}, u32[]{:S(2)}) async-start(f32[16,1024,4]{1,2,0:T(4,128)} %broadcast_in_dim.26), calls=%async_computation.2 | async-start | bytes 524288 | tf_op jit(solution)/shard_map/all_to_all | solution.py:41
  526.4 40.7 %all-to-all-start = ((f32[16,1536,4]{1,2,0:T(4,128)}), f32[16,1536,4]{1,2,0:T(4,128)S(1)}, u32[]{:S(2)}, u32[]{:S(2)}) async-start(f32[16,1536,4]{1,2,0:T(4,128)} %broadcast_in_dim.25), calls=%async_computation | async-start | bytes 786432 | tf_op jit(solution)/shard_map/all_to_all | solution.py:41
  568.7 18.7 %all-to-all-start.10 = ((f32[16,1536,4]{1,2,0:T(4,128)}), f32[16,1536,4]{1,2,0:T(4,128)}, u32[]{:S(2)}, u32[]{:S(2)}) async-start(f32[16,1536,4]{1,2,0:T(4,128)} %broadcast_in_dim.31), calls=%async_computation.10 | async-start | bytes 786432 | tf_op jit(solution)/shard_map/all_to_all | solution.py:41
  588.9 13.9 %all-to-all-start.11 = ((f32[16,1536,4]{1,2,0:T(4,128)}), f32[16,1536,4]{1,2,0:T(4,128)S(1)}, u32[]{:S(2)}, u32[]{:S(2)}) async-start(f32[16,1536,4]{1,2,0:T(4,128)} %broadcast_in_dim.32), calls=%async_computation.11 | async-start | bytes 786432 | tf_op jit(solution)/shard_map/all_to_all | solution.py:41
  604.4 12.9 %all-to-all-start.9 = ((f32[16,1536,4]{1,2,0:T(4,128)}), f32[16,1536,4]{1,2,0:T(4,128)S(1)}, u32[]{:S(2)}, u32[]{:S(2)}) async-start(f32[16,1536,4]{1,2,0:T(4,128)} %broadcast_in_dim.30), calls=%async_computation.9 | async-start | bytes 786432 | tf_op jit(solution)/shard_map/all_to_all | solution.py:41
  608.1 191.9 %reduce-scatter.2.cloned.1.call-start = ((), (), s32[]{:S(2)}) async-start(), calls=%async_computation.25 | async-start | bytes 8257536 | tf_op jit(solution)/shard_map/reduce_scatter | solution.py:257
  614.7 35.7 %collective-permute-start = (bf16[4,512,4,128]{1,3,2,0:T(8,128)(2,1)}, bf16[4,512,4,128]{1,3,2,0:T(8,128)(2,1)}, u32[]{:S(2)}, u32[]{:S(2)}) collective-permute-start(bf16[4,512,4,128]{1,3,2,0:T(8,128)(2,1)} %pad_maximum_fusion), channel_id=1, source_target_pairs={{0,64},{1,65},{2,66},{3,67},{4,68},{5,69},{6,70},{7,71},{8,72},{9,... | collective-permute-start | bytes 6291464 | tf_op jit(solution)/shard_map/ppermute | solution.py:96
  700.4 14.4 %all-to-all-start.14 = ((f32[16,1,128]{2,1,0:T(1,128)}), f32[16,1,128]{2,1,0:T(1,128)S(1)}, u32[]{:S(2)}, u32[]{:S(2)}) async-start(f32[16,1,128]{2,1,0:T(1,128)} %reshape.528), calls=%async_computation.15 | async-start | bytes 16384 | tf_op jit(solution)/shard_map/all_to_all | solution.py:82
  714.9 10.9 %all-to-all-start.16 = ((f32[16,1,128]{2,1,0:T(1,128)}), f32[16,1,128]{2,1,0:T(1,128)S(1)}, u32[]{:S(2)}, u32[]{:S(2)}) async-start(f32[16,1,128]{2,1,0:T(1,128)} %reshape.524), calls=%async_computation.17 | async-start | bytes 16384 | tf_op jit(solution)/shard_map/all_to_all | solution.py:82
  754.6 11.0 %all-to-all-start.19 = ((f32[16,1,128]{2,1,0:T(1,128)}), f32[16,1,128]{2,1,0:T(1,128)S(1)}, u32[]{:S(2)}, u32[]{:S(2)}) async-start(f32[16,1,128]{2,1,0:T(1,128)} %reshape.522), calls=%async_computation.20 | async-start | bytes 16384 | tf_op jit(solution)/shard_map/all_to_all | solution.py:82
  765.6 10.9 %all-to-all-start.17 = ((f32[16,1,128]{2,1,0:T(1,128)}), f32[16,1,128]{2,1,0:T(1,128)S(1)}, u32[]{:S(2)}, u32[]{:S(2)}) async-start(f32[16,1,128]{2,1,0:T(1,128)} %reshape.526), calls=%async_computation.18 | async-start | bytes 16384 | tf_op jit(solution)/shard_map/all_to_all | solution.py:82
  776.5 11.0 %all-to-all-start.15 = ((f32[16,1,128]{2,1,0:T(1,128)}), f32[16,1,128]{2,1,0:T(1,128)S(1)}, u32[]{:S(2)}, u32[]{:S(2)}) async-start(f32[16,1,128]{2,1,0:T(1,128)} %reshape.530), calls=%async_computation.16 | async-start | bytes 16384 | tf_op jit(solution)/shard_map/all_to_all | solution.py:82
  787.5 10.9 %all-to-all-start.13 = ((f32[16,1,128]{2,1,0:T(1,128)}), f32[16,1,128]{2,1,0:T(1,128)S(1)}, u32[]{:S(2)}, u32[]{:S(2)}) async-start(f32[16,1,128]{2,1,0:T(1,128)} %reshape.534), calls=%async_computation.14 | async-start | bytes 16384 | tf_op jit(solution)/shard_map/all_to_all | solution.py:82
  (38 other events, 672.2 us)
Sparse Core Ops, SparseCore 0:
  89.5 112.7 all-gather.4
  204.0 100.5 all-gather.8
  306.2 77.0 all-gather.6
  384.9 67.3 all-gather.10
  699.1 46.4 reduce-scatter.1
